TPU v7x, 32 devices: a whole 2x2x4 slice. The times are simulated.
32 devices in a mesh: rep: 8 (over z, y), ep: 4 (over x, core).
Axes of the slice: x: 2, y: 2, z: 4, core: 2. Of those that a mesh axis runs over, the one named last changes fastest.
Arguments:
- tokens: bfloat16 [16384, 1536], P(('rep', 'ep')), may hold values from -6 to 6
- norm_attn: bfloat16 [1536], replicated, may hold values from 0.099609375 to 1.8984375
- w_query: bfloat16 [1536, 1536], replicated, may hold values from -0.15625 to 0.15625
- key_projection: bfloat16 [1536, 512], replicated, may hold values from -0.15625 to 0.15625
- value_projection: bfloat16 [1536, 512], replicated, may hold values from -0.15625 to 0.15625
- w_out: bfloat16 [1536, 1536], replicated, may hold values from -2.5 to 2.5
- norm_ffn: bfloat16 [1536], replicated, may hold values from 0.099609375 to 1.8984375
- w_router: bfloat16 [1536, 20], replicated, may hold values from -0.078125 to 0.078125
- w_gate: bfloat16 [20, 1536, 512], P('ep'), may hold values from -0.15625 to 0.15625
- w_up: bfloat16 [20, 1536, 512], P('ep'), may hold values from -0.15625 to 0.15625
- w_down: bfloat16 [20, 512, 1536], P('ep'), may hold values from -3 to 3
- routes: int32 [16384, 8], P(('rep', 'ep')), may hold values from 0 to 19, as said below
- cotangent: bfloat16 [16384, 1536], P(('rep', 'ep')), may hold values from -6 to 6
Outputs:
- mixed: bfloat16 [16384, 1536], P(('rep', 'ep'))
- d_input: float32 [16384, 1536], P(('rep', 'ep'))
- grad_norm_attn: float32 [1536], P('ep')
- grad_query: float32 [1536, 1536], P('ep')
- grad_key: float32 [1536, 512], P('ep')
- grad_value: float32 [1536, 512], P('ep')
- grad_out: float32 [1536, 1536], P('ep')
- grad_norm_ffn: float32 [1536], P('ep')
- grad_router: float32 [1536, 20], P('ep')
- grad_gate: float32 [20, 1536, 512], P('ep')
- grad_up: float32 [20, 1536, 512], P('ep')
- grad_down: float32 [20, 512, 1536], P('ep')
Inputs may be any that keep to these rules, and one draw needn't show every extreme that they name: `routes`: each row names 8 different experts. In each aligned block of 512 rows (the rows of one device) no expert is named by more than 384 rows, and in each group of 4 consecutive such blocks one expert is named by exactly 384 rows of every block of the group.
All inputs are finite; a program needn't handle non-finite values.
Results may differ from a plain program's by a relative error of at most 0.02.
Values may be sent and summed in bfloat16 or wider, within the bound.
A program may use at most 448 MiB of HBM per device.

v0:
```python
import math
import jax
import jax.numpy as jnp
from jax import lax
from jax.sharding import PartitionSpec as P

QUERY_HEADS = 24
KEY_VALUE_HEADS = 8
HEAD_SIZE = 64
TOPK = 8
SEQUENCE_TOKENS = 512
BLOCK = 256
CAP = 384
epsilon = 1e-06
masked_value = -1e30


def rope_tables(token_count, width):
    half_width = width // 2
    places = (jnp.arange(token_count) % SEQUENCE_TOKENS).astype(jnp.float32)
    rates = jnp.exp(jnp.arange(half_width, dtype=jnp.float32) * (-2.0 * math.log(10000.0) / width))
    angles = places[:, None] * rates[None, :]
    return (jnp.cos(angles)[:, None, :], jnp.sin(angles)[:, None, :])


def apply_rotary(field, cosine_table, sine_table):
    half_width = field.shape[-1] // 2
    first = field[..., :half_width]
    second = field[..., half_width:]
    return jnp.concatenate(
        [first * cosine_table - second * sine_table, second * cosine_table + first * sine_table], -1
    )


def invert_rotary(field, cosine_table, sine_table):
    half_width = field.shape[-1] // 2
    first = field[..., :half_width]
    second = field[..., half_width:]
    return jnp.concatenate(
        [first * cosine_table + second * sine_table, second * cosine_table - first * sine_table], -1
    )


def norm_forward(field, gain):
    inverse = lax.rsqrt(jnp.mean(field * field, -1, keepdims=True) + epsilon)
    normal = field * inverse
    return ((normal * gain.astype(jnp.float32)).astype(jnp.bfloat16), normal, inverse)


def norm_backward(d_normed, normal, inverse, gain):
    scaled = d_normed * gain.astype(jnp.float32)
    d_field = inverse * (scaled - normal * jnp.mean(scaled * normal, -1, keepdims=True))
    return (d_field, jnp.sum(d_normed * normal, 0))


def score_block(queries, key_rows):
    places = jnp.arange(SEQUENCE_TOKENS) // BLOCK
    allowed = places[None, :] <= places[:, None]
    scores = jnp.einsum(
        "qhgd,khd->hgqk", queries, key_rows, preferred_element_type=jnp.float32
    ) * HEAD_SIZE ** (-0.5)
    return jnp.where(allowed, scores, masked_value)


def attend(pack):
    queries, key_rows, value_rows = pack
    scores = score_block(queries, key_rows)
    highest = jnp.max(scores, -1, keepdims=True)
    shifted = jnp.exp(scores - highest)
    totals = jnp.sum(shifted, -1, keepdims=True)
    probs_bf = (shifted / totals).astype(jnp.bfloat16)
    head_mix = jnp.einsum(
        "hgqk,khd->qhgd", probs_bf, value_rows, preferred_element_type=jnp.float32
    )
    return (head_mix.astype(jnp.bfloat16), highest + jnp.log(totals))


def attend_back(pack):
    queries, key_rows, value_rows, d_mix, log_totals = pack
    factor = HEAD_SIZE ** (-0.5)
    scores = score_block(queries, key_rows)
    probs_f = jnp.exp(scores - log_totals)
    probs_bf = probs_f.astype(jnp.bfloat16)
    d_probs = jnp.einsum("qhgd,khd->hgqk", d_mix, value_rows, preferred_element_type=jnp.float32)
    centre = jnp.sum(probs_f * d_probs, -1, keepdims=True)
    d_scores = (probs_f * (d_probs - centre)).astype(jnp.bfloat16)
    d_queries = (
        jnp.einsum("hgqk,khd->qhgd", d_scores, key_rows, preferred_element_type=jnp.float32)
        * factor
    )
    d_keys = (
        jnp.einsum("hgqk,qhgd->khd", d_scores, queries, preferred_element_type=jnp.float32) * factor
    )
    d_values = jnp.einsum("hgqk,qhgd->khd", probs_bf, d_mix, preferred_element_type=jnp.float32)
    return (d_queries, d_keys, d_values)


def expert_forward(rows, gate_w, up_w, down_w):
    gate_pre = jnp.einsum("erd,edf->erf", rows, gate_w, preferred_element_type=jnp.float32)
    up_pre = jnp.einsum("erd,edf->erf", rows, up_w, preferred_element_type=jnp.float32)
    hidden = (jax.nn.silu(gate_pre) * up_pre).astype(jnp.bfloat16)
    result = jnp.einsum("erf,efd->erd", hidden, down_w, preferred_element_type=jnp.float32).astype(
        jnp.bfloat16
    )
    return (result, gate_pre, up_pre, hidden)


def expert_backward(rows, gate_w, up_w, down_w, gate_pre, up_pre, hidden, d_result):
    d_hidden = jnp.einsum("erd,efd->erf", d_result, down_w, preferred_element_type=jnp.float32)
    grad_down = jnp.einsum("erf,erd->efd", hidden, d_result, preferred_element_type=jnp.float32)
    sigma = jax.nn.sigmoid(gate_pre)
    swish = gate_pre * sigma
    d_gate_pre = (d_hidden * up_pre * sigma * (1.0 + gate_pre * (1.0 - sigma))).astype(jnp.bfloat16)
    d_up_pre = (d_hidden * swish).astype(jnp.bfloat16)
    grad_gate = jnp.einsum("erd,erf->edf", rows, d_gate_pre, preferred_element_type=jnp.float32)
    grad_up = jnp.einsum("erd,erf->edf", rows, d_up_pre, preferred_element_type=jnp.float32)
    d_rows = jnp.einsum("erf,edf->erd", d_gate_pre, gate_w, preferred_element_type=jnp.float32)
    d_rows = d_rows + jnp.einsum("erf,edf->erd", d_up_pre, up_w, preferred_element_type=jnp.float32)
    return (d_rows.astype(jnp.bfloat16), grad_gate, grad_up, grad_down)


def pack_rows(rows, target, experts_all, width):
    buffer = jnp.zeros((experts_all * CAP, width), jnp.bfloat16).at[target].set(rows)
    return buffer.reshape(experts_all, CAP, width)


def unpack_rows(buffer, target, token_count, width):
    return buffer.reshape(-1, width)[target].reshape(token_count, TOPK, width)


def per_device(
    tokens,
    norm_attn,
    w_query,
    key_projection,
    value_projection,
    w_out,
    norm_ffn,
    w_router,
    w_gate,
    w_up,
    w_down,
    routes,
    cotangent,
):
    token_count = tokens.shape[0]
    width = tokens.shape[1]
    experts_all = w_router.shape[1]
    query_groups = QUERY_HEADS // KEY_VALUE_HEADS
    sequence_total = token_count // SEQUENCE_TOKENS
    x_float = tokens.astype(jnp.float32)
    hidden_first, normal_one, inverse_one = norm_forward(x_float, norm_attn)
    query_unrotated = jnp.dot(hidden_first, w_query, preferred_element_type=jnp.float32)
    key_unrotated = jnp.dot(hidden_first, key_projection, preferred_element_type=jnp.float32)
    value_row_block = jnp.dot(
        hidden_first, value_projection, preferred_element_type=jnp.float32
    ).astype(jnp.bfloat16)
    cosine_table, sine_table = rope_tables(token_count, HEAD_SIZE)
    query_rotated = apply_rotary(
        query_unrotated.reshape(token_count, QUERY_HEADS, HEAD_SIZE), cosine_table, sine_table
    ).astype(jnp.bfloat16)
    key_rotated = apply_rotary(
        key_unrotated.reshape(token_count, KEY_VALUE_HEADS, HEAD_SIZE), cosine_table, sine_table
    ).astype(jnp.bfloat16)
    query_sequence = query_rotated.reshape(
        sequence_total, SEQUENCE_TOKENS, KEY_VALUE_HEADS, query_groups, HEAD_SIZE
    )
    key_sequence = key_rotated.reshape(sequence_total, SEQUENCE_TOKENS, KEY_VALUE_HEADS, HEAD_SIZE)
    value_sequence = value_row_block.reshape(
        sequence_total, SEQUENCE_TOKENS, KEY_VALUE_HEADS, HEAD_SIZE
    )
    attn_seq, log_totals = lax.map(attend, (query_sequence, key_sequence, value_sequence))
    attn_flat = attn_seq.reshape(token_count, QUERY_HEADS * HEAD_SIZE)
    branch = jnp.dot(attn_flat, w_out, preferred_element_type=jnp.float32)
    resid = x_float + branch
    h_two, normal_two, inverse_two = norm_forward(resid, norm_ffn)
    logits = jnp.dot(h_two, w_router, preferred_element_type=jnp.float32)
    router_probs = jax.nn.softmax(logits, -1)
    expert_ids = jnp.arange(experts_all)
    choose = (routes[:, :, None] == expert_ids[None, None, :]).astype(jnp.float32)
    gates = jnp.sum(choose * router_probs[:, None, :], -1)
    flat_routes = routes.reshape(-1)
    matches = (flat_routes[:, None] == expert_ids[None, :]).astype(jnp.int32)
    slot_of = jnp.sum((jnp.cumsum(matches, 0) - 1) * matches, 1)
    target = flat_routes * CAP + slot_of
    send_buf = pack_rows(jnp.repeat(h_two, TOPK, axis=0), target, experts_all, width)
    recv_rows = lax.all_to_all(send_buf, "ep", split_axis=0, concat_axis=1, tiled=True)
    y_buf, gate_pre, up_pre, hidden = expert_forward(recv_rows, w_gate, w_up, w_down)
    back_y = lax.all_to_all(y_buf, "ep", split_axis=1, concat_axis=0, tiled=True)
    y_rows = unpack_rows(back_y, target, token_count, width)
    moe_sum = jnp.sum(gates[:, :, None] * y_rows.astype(jnp.float32), 1)
    mixed = (resid + moe_sum).astype(jnp.bfloat16)
    d_out = cotangent.astype(jnp.float32)
    d_gates = jnp.einsum("tkd,td->tk", y_rows, cotangent, preferred_element_type=jnp.float32)
    d_router = jnp.sum(choose * d_gates[:, :, None], 1)
    d_logits = (
        router_probs * (d_router - jnp.sum(router_probs * d_router, -1, keepdims=True))
    ).astype(jnp.bfloat16)
    grad_router = jnp.einsum("td,te->de", h_two, d_logits, preferred_element_type=jnp.float32)
    d_htwo = jnp.einsum("te,de->td", d_logits, w_router, preferred_element_type=jnp.float32)
    d_y = (
        (gates[:, :, None] * d_out[:, None, :])
        .astype(jnp.bfloat16)
        .reshape(token_count * TOPK, width)
    )
    d_send = pack_rows(d_y, target, experts_all, width)
    d_recv = lax.all_to_all(d_send, "ep", split_axis=0, concat_axis=1, tiled=True)
    d_rows_held, grad_gate, grad_up, grad_down = expert_backward(
        recv_rows, w_gate, w_up, w_down, gate_pre, up_pre, hidden, d_recv
    )
    back_rows = lax.all_to_all(d_rows_held, "ep", split_axis=1, concat_axis=0, tiled=True)
    d_htwo = d_htwo + jnp.sum(
        unpack_rows(back_rows, target, token_count, width).astype(jnp.float32), 1
    )
    d_resid_norm, grad_norm_ffn = norm_backward(d_htwo, normal_two, inverse_two, norm_ffn)
    d_resid = d_out + d_resid_norm
    d_branch = d_resid.astype(jnp.bfloat16)
    grad_out = jnp.einsum("ta,td->ad", attn_flat, d_branch, preferred_element_type=jnp.float32)
    attention_gradient = jnp.einsum(
        "td,ad->ta", d_branch, w_out, preferred_element_type=jnp.float32
    ).astype(jnp.bfloat16)
    attention_gradient = attention_gradient.reshape(
        sequence_total, SEQUENCE_TOKENS, KEY_VALUE_HEADS, query_groups, HEAD_SIZE
    )
    d_q_rot, rotated_key_gradient, value_sequence_gradient = lax.map(
        attend_back, (query_sequence, key_sequence, value_sequence, attention_gradient, log_totals)
    )
    d_q_pre = (
        invert_rotary(
            d_q_rot.reshape(token_count, QUERY_HEADS, HEAD_SIZE), cosine_table, sine_table
        )
        .reshape(token_count, QUERY_HEADS * HEAD_SIZE)
        .astype(jnp.bfloat16)
    )
    d_k_pre = (
        invert_rotary(
            rotated_key_gradient.reshape(token_count, KEY_VALUE_HEADS, HEAD_SIZE),
            cosine_table,
            sine_table,
        )
        .reshape(token_count, KEY_VALUE_HEADS * HEAD_SIZE)
        .astype(jnp.bfloat16)
    )
    value_rows_gradient = value_sequence_gradient.reshape(
        token_count, KEY_VALUE_HEADS * HEAD_SIZE
    ).astype(jnp.bfloat16)
    grad_query = jnp.einsum("td,tq->dq", hidden_first, d_q_pre, preferred_element_type=jnp.float32)
    grad_key = jnp.einsum("td,tq->dq", hidden_first, d_k_pre, preferred_element_type=jnp.float32)
    grad_value = jnp.einsum(
        "td,tq->dq", hidden_first, value_rows_gradient, preferred_element_type=jnp.float32
    )
    d_hone = jnp.einsum("tq,dq->td", d_q_pre, w_query, preferred_element_type=jnp.float32)
    d_hone = d_hone + jnp.einsum(
        "tq,dq->td", d_k_pre, key_projection, preferred_element_type=jnp.float32
    )
    d_hone = d_hone + jnp.einsum(
        "tq,dq->td", value_rows_gradient, value_projection, preferred_element_type=jnp.float32
    )
    d_x_norm, grad_norm_attn = norm_backward(d_hone, normal_one, inverse_one, norm_attn)
    d_input = d_resid + d_x_norm
    part_na, part_q, part_k, part_v, part_o, part_nf, part_r = (
        lax.psum_scatter(
            grad_norm_attn.astype(jnp.bfloat16), "ep", scatter_dimension=0, tiled=True
        ).astype(jnp.float32),
        lax.psum_scatter(
            grad_query.astype(jnp.bfloat16), "ep", scatter_dimension=0, tiled=True
        ).astype(jnp.float32),
        lax.psum_scatter(
            grad_key.astype(jnp.bfloat16), "ep", scatter_dimension=0, tiled=True
        ).astype(jnp.float32),
        lax.psum_scatter(
            grad_value.astype(jnp.bfloat16), "ep", scatter_dimension=0, tiled=True
        ).astype(jnp.float32),
        lax.psum_scatter(
            grad_out.astype(jnp.bfloat16), "ep", scatter_dimension=0, tiled=True
        ).astype(jnp.float32),
        lax.psum_scatter(
            grad_norm_ffn.astype(jnp.bfloat16), "ep", scatter_dimension=0, tiled=True
        ).astype(jnp.float32),
        lax.psum_scatter(
            grad_router.astype(jnp.bfloat16), "ep", scatter_dimension=0, tiled=True
        ).astype(jnp.float32),
    )
    part_gate, part_up, part_down = (grad_gate, grad_up, grad_down)
    sum_na, sum_q, sum_k, sum_v, sum_o, sum_nf, sum_r = lax.psum(
        (part_na, part_q, part_k, part_v, part_o, part_nf, part_r), "rep"
    )
    share_gate, share_up, share_down = (
        lax.psum_scatter(part_gate, "rep", scatter_dimension=1, tiled=True),
        lax.psum_scatter(part_up, "rep", scatter_dimension=1, tiled=True),
        lax.psum_scatter(part_down, "rep", scatter_dimension=2, tiled=True),
    )
    full_gate, full_up, full_down = (
        lax.all_gather(share_gate.astype(jnp.bfloat16), "rep", axis=1, tiled=True).astype(
            share_gate.dtype
        ),
        lax.all_gather(share_up.astype(jnp.bfloat16), "rep", axis=1, tiled=True).astype(
            share_up.dtype
        ),
        lax.all_gather(share_down.astype(jnp.bfloat16), "rep", axis=2, tiled=True).astype(
            share_down.dtype
        ),
    )
    return (
        mixed,
        d_input,
        sum_na,
        sum_q,
        sum_k,
        sum_v,
        sum_o,
        sum_nf,
        sum_r,
        full_gate,
        full_up,
        full_down,
    )


def solution(mesh):
    placed = (
        P(("rep", "ep"), None),
        P(),
        P(),
        P(),
        P(),
        P(),
        P(),
        P(),
        P("ep", None, None),
        P("ep", None, None),
        P("ep", None, None),
        P(("rep", "ep"), None),
        P(("rep", "ep"), None),
    )
    return jax.shard_map(
        per_device,
        mesh=mesh,
        in_specs=placed,
        out_specs=(
            P(("rep", "ep"), None),
            P(("rep", "ep"), None),
            P("ep"),
            P("ep", None),
            P("ep", None),
            P("ep", None),
            P("ep", None),
            P("ep"),
            P("ep", None),
            P("ep", None, None),
            P("ep", None, None),
            P("ep", None, None),
        ),
        check_vma=False,
    )
```

profile of v0, /device:TPU:0, one launch (start us, length us, event | category | flops | bytes accessed | tf_op | source)
XLA Modules:
  0.0 2776.9 jit_solution(4677663683264362506)
XLA Ops:
  74.2 32.5 %scatter_custom_fusion = bf16[7680,1536]{1,0:T(8,128)(2,1)} fusion(s32[4096]{0:T(1024)S(1)} %bitcast.201, bf16[]{:T(256)} %constant.121.clone.1, bf16[512,1536]{1,0:T(8,128)(2,1)S(1)} %multiply_convert_fusion.3), kind=kCustom, calls=%fused_computation.29 | custom fusion | bytes 25165826 | tf_op jit(solution)/shard_map/scatter | solution.py:123
  106.7 262.0 %all_to_all.66 = bf16[20,384,1536]{2,1,0:T(8,128)(2,1)S(1)} all-to-all(bf16[20,384,1536]{2,1,0:T(8,128)(2,1)} %bitcast.173), channel_id=1, replica_groups=mesh['rep'=8,'ep'=4] {'ep'}, dimensions={0} | all-to-all | bytes 47185920 | tf_op jit(solution)/shard_map/all_to_all | solution.py:187
  376.7 22.3 fusion.71
  399.0 29.6 %multiply_convert_fusion.2 = (bf16[5,1536,512]{2,1,0:T(8,128)(2,1)}, f32[5,1536,512]{2,1,0:T(8,128)}) fusion(f32[5,1536,512]{2,1,0:T(8,128)} %fusion.71, bf16[5,1536,1536]{2,1,0:T(8,128)(2,1)} %bitcast.175, bf16[5,1536,512]{2,1,0:T(8,128)(2,1)} %param.22), kind=kOutput, calls=%fused_computation.23 | convolution fusion | flops 12103188480 | bytes 70778880 | tf_op jit(solution)/shard_map/erd,edf->erf/dot_general | solution.py:100
  448.5 27.3 copy.92
  491.3 402.7 %all-to-all-done.1 = bf16[5,1536,1536]{2,0,1:T(8,128)(2,1)} async-done(((bf16[5,1536,1536]{2,0,1:T(8,128)(2,1)}), bf16[5,1536,1536]{2,0,1:T(8,128)(2,1)}, u32[]{:S(2)}, u32[]{:S(2)}) %all-to-all-start.1) | async-done | bytes 23592992 | tf_op jit(solution)/shard_map/all_to_all | solution.py:189
  894.1 28.5 %copy.93 = bf16[5,4,384,1536]{3,2,0,1:T(8,128)(2,1)} copy(bf16[5,4,384,1536]{3,0,2,1:T(8,128)(2,1)} %bitcast.20) | data formatting | bytes 47185920 | tf_op jit(solution)/shard_map/all_to_all | solution.py:189
  922.6 36.2 %gather_fusion = bf16[4096,1536]{1,0:T(8,128)(2,1)} fusion(bf16[7680,1536]{1,0:T(8,128)(2,1)} %bitcast.169, s32[4096]{0:T(1024)S(1)} %broadcast_clamp_fusion), kind=kCustom, calls=%fused_computation | custom fusion | bytes 25182208 | tf_op jit(solution)/shard_map/gather | solution.py:128
  976.4 33.3 %scatter_custom_fusion.1 = bf16[7680,1536]{1,0:T(8,128)(2,1)} fusion(s32[4096]{0:T(1024)S(1)} %bitcast.203, bf16[4096,1536]{1,0:T(8,128)(2,1)} %fusion.3, bf16[]{:T(256)} %constant.121.clone.1), kind=kCustom, calls=%fused_computation.33 | custom fusion | bytes 23593472 | tf_op jit(solution)/shard_map/scatter | solution.py:123
  1009.8 261.4 %all_to_all.67 = bf16[20,384,1536]{2,1,0:T(8,128)(2,1)S(1)} all-to-all(bf16[20,384,1536]{2,1,0:T(8,128)(2,1)} %bitcast.170), channel_id=1, replica_groups=mesh['rep'=8,'ep'=4] {'ep'}, dimensions={0} | all-to-all | bytes 47185920 | tf_op jit(solution)/shard_map/all_to_all | solution.py:207
  1300.3 29.0 %multiply_convert_fusion = (bf16[5,1536,512]{2,1,0:T(8,128)(2,1)}, bf16[5,1536,512]{2,1,0:T(8,128)(2,1)}) fusion(f32[5,1536,512]{2,1,0:T(8,128)} %fusion.71, f32[5,1536,512]{2,1,0:T(8,128)} %get-tuple-element.139, bf16[5,1536,1536]{2,1,0:T(8,128)(2,1)} %bitcast.179, bf16[5,512,1536]{2,1,0:T(8,128)(2,1)} %param.23), kind=kOutput, calls=%fused_computation.21 | convolution fusion | flops 12130713600 | bytes 78643200 | tf_op jit(solution)/shard_map/erd,efd->erf/dot_general | solution.py:109
  1373.0 24.3 fusion.72
  1397.3 30.6 %add_convert_fusion = bf16[5,1536,1536]{2,1,0:T(8,128)(2,1)} fusion(f32[5,1536,1536]{2,1,0:T(8,128)} %fusion.72, bf16[5,1536,512]{2,1,0:T(8,128)(2,1)} %get-tuple-element.120, bf16[5,1536,512]{2,1,0:T(8,128)(2,1)} %param.22), kind=kOutput, calls=%fused_computation.4 | convolution fusion | flops 12103188480 | bytes 86507520 | tf_op jit(solution)/shard_map/erf,edf->erd/dot_general | solution.py:118
  1427.9 27.3 copy.96
  1484.9 390.5 %all-to-all-done.3 = bf16[5,1536,1536]{2,0,1:T(8,128)(2,1)} async-done(((bf16[5,1536,1536]{2,0,1:T(8,128)(2,1)}), bf16[5,1536,1536]{2,0,1:T(8,128)(2,1)}, u32[]{:S(2)}, u32[]{:S(2)}) %all-to-all-start.3) | async-done | bytes 23592992 | tf_op jit(solution)/shard_map/all_to_all | solution.py:211
  1875.5 28.9 %copy.97 = bf16[5,4,384,1536]{3,2,0,1:T(8,128)(2,1)} copy(bf16[5,4,384,1536]{3,0,2,1:T(8,128)(2,1)} %bitcast.31) | data formatting | bytes 47185920 | tf_op jit(solution)/shard_map/all_to_all | solution.py:211
  1904.4 36.1 %gather_fusion.1 = bf16[4096,1536]{1,0:T(8,128)(2,1)} fusion(bf16[7680,1536]{1,0:T(8,128)(2,1)} %bitcast.168, s32[4096]{0:T(1024)S(1)} %copy-done.42), kind=kCustom, calls=%fused_computation.1 | custom fusion | bytes 25182208 | tf_op jit(solution)/shard_map/gather | solution.py:128
  1998.6 22.7 fusion.2
  2114.4 31.3 %reduce-scatter.13.cloned.1.call-done = bf16[384,512]{1,0:T(8,128)(2,1)} async-done(((bf16[1536,512]{1,0:T(8,128)(2,1)}), bf16[384,512]{1,0:T(8,128)(2,1)}) %reduce-scatter.13.cloned.1.call-update) | async-done | bytes 393232 | tf_op jit(solution)/shard_map/reduce_scatter | solution.py:268
  2145.7 50.4 %reduce-scatter.17.cloned.1.call-done = bf16[384,1536]{1,0:T(8,128)(2,1)} async-done(((bf16[1536,1536]{1,0:T(8,128)(2,1)}), bf16[384,1536]{1,0:T(8,128)(2,1)}) %reduce-scatter.17.cloned.1.call-update) | async-done | bytes 1179664 | tf_op jit(solution)/shard_map/reduce_scatter | solution.py:274
  2196.1 50.6 %reduce-scatter.11.cloned.1.call-done = bf16[384,1536]{1,0:T(8,128)(2,1)} async-done(((bf16[1536,1536]{1,0:T(8,128)(2,1)}), bf16[384,1536]{1,0:T(8,128)(2,1)}) %reduce-scatter.11.cloned.1.call-update) | async-done | bytes 1179664 | tf_op jit(solution)/shard_map/reduce_scatter | solution.py:265
  2246.6 310.2 %all-reduce.5 = (f32[384]{0:T(512)}, f32[384,1536]{1,0:T(8,128)}, f32[384,512]{1,0:T(8,128)}, f32[384,512]{1,0:T(8,128)}, f32[384,1536]{1,0:T(8,128)}, /*index=5*/f32[384]{0:T(512)}, f32[384,20]{0,1:T(8,128)}) all-reduce(f32[384]{0:T(512)S(1)} %get-tuple-element.147, ...), channel_id=1, replica_groups=mesh['rep'=8,'ep'=4] {'rep'}, use_global_device_ids=true, to_apply=%region_21.22 | all-reduce | flops 1581312 | bytes 9489408 | tf_op jit(solution)/shard_map/psum | solution.py:285
  2568.3 71.0 %all-gather.6.cloned.1.call-done = bf16[5,1536,512]{2,1,0:T(8,128)(2,1)} async-done(((bf16[5,192,512]{2,1,0:T(8,128)(2,1)}), bf16[5,1536,512]{2,1,0:T(8,128)(2,1)}) %all-gather.6.cloned.1.call-update) | async-done | bytes 7864336 | tf_op jit(solution)/shard_map/all_gather | solution.py:297
  2650.9 107.8 %all-gather.4.cloned.1.call-done = bf16[5,1536,512]{2,1,0:T(8,128)(2,1)} async-done(((bf16[5,192,512]{2,1,0:T(8,128)(2,1)}), bf16[5,1536,512]{2,1,0:T(8,128)(2,1)}) %all-gather.4.cloned.1.call-update) | async-done | bytes 7864336 | tf_op jit(solution)/shard_map/all_gather | solution.py:294
  (250 shorter events, 414.4 us)
Async XLA Ops:
  12.5 59.9 %copy-start.43 = (f32[1536]{0:T(1024)}, f32[1536]{0:T(1024)S(1)}, u32[]{:S(2)}) copy-start(f32[1536]{0:T(1024)S(1)} %convert_element_type.213) | copy-start | bytes 18436
  13.0 43.9 %copy-start.12 = (pred[512,512]{0,1:T(8,128)(4,1)}, pred[512,512]{0,1:T(8,128)(4,1)S(1)}, u32[]{:S(2)}) copy-start(pred[512,512]{0,1:T(8,128)(4,1)S(1)} %broadcast_compare_fusion) | copy-start | bytes 786436
  29.9 27.0 copy-start.34
  45.5 23.6 slice-start
  72.2 34.5 %copy-start.49 = (f32[512]{0:T(512)}, f32[512]{0:T(512)S(1)}, u32[]{:S(2)}) copy-start(f32[512]{0:T(512)S(1)} %add_rsqrt_fusion) | copy-start | bytes 6148
  74.2 415.9 %copy-start.3 = (bf16[512,1536]{1,0:T(8,128)(2,1)}, bf16[512,1536]{1,0:T(8,128)(2,1)S(1)}, u32[]{:S(2)}) copy-start(bf16[512,1536]{1,0:T(8,128)(2,1)S(1)} %multiply_convert_fusion.3) | copy-start | bytes 4718596
  475.8 418.3 %all-to-all-start.1 = ((bf16[5,1536,1536]{2,0,1:T(8,128)(2,1)}), bf16[5,1536,1536]{2,0,1:T(8,128)(2,1)}, u32[]{:S(2)}, u32[]{:S(2)}) async-start(bf16[5,1536,1536]{2,0,1:T(8,128)(2,1)} %copy.92), calls=%async_computation.1 | async-start | bytes 75497472 | tf_op jit(solution)/shard_map/all_to_all | solution.py:189
  486.3 1569.1 %reduce-scatter.23.cloned.1.call-start = ((), (), s32[]{:S(2)}) async-start(), calls=%async_computation.20 | async-start | bytes 17694720 | tf_op jit(solution)/shard_map/reduce_scatter | solution.py:291
  490.7 431.9 %copy-start.47 = (f32[512]{0:T(512)}, f32[512]{0:T(512)S(1)}, u32[]{:S(2)}) copy-start(f32[512]{0:T(512)S(1)} %get-tuple-element.140) | copy-start | bytes 6148
  490.8 431.8 %copy-start.51 = (f32[512]{0:T(512)}, f32[512]{0:T(512)S(1)}, u32[]{:S(2)}) copy-start(f32[512]{0:T(512)S(1)} %fusion.47) | copy-start | bytes 6148
  491.3 431.3 %copy-start.41 = (s32[4096]{0:T(1024)}, s32[4096]{0:T(1024)S(1)}, u32[]{:S(2)}) copy-start(s32[4096]{0:T(1024)S(1)} %broadcast_clamp_fusion) | copy-start | bytes 49156
  922.6 36.2 %copy-start.10 = (bf16[512,1536]{1,0:T(8,128)(2,1)S(1)}, bf16[512,1536]{1,0:T(8,128)(2,1)}, u32[]{:S(2)}) copy-start(bf16[512,1536]{1,0:T(8,128)(2,1)} %param.25) | copy-start | bytes 4718596
  1300.2 757.9 %reduce-scatter.21.cloned.1.call-start = ((), (), s32[]{:S(2)}) async-start(), calls=%async_computation.18 | async-start | bytes 17694720 | tf_op jit(solution)/shard_map/reduce_scatter | solution.py:290
  1351.0 710.4 %reduce-scatter.19.cloned.1.call-start = ((), (), s32[]{:S(2)}) async-start(), calls=%async_computation.16 | async-start | bytes 17694720 | tf_op jit(solution)/shard_map/reduce_scatter | solution.py:289
  1455.2 420.2 %all-to-all-start.3 = ((bf16[5,1536,1536]{2,0,1:T(8,128)(2,1)}), bf16[5,1536,1536]{2,0,1:T(8,128)(2,1)}, u32[]{:S(2)}, u32[]{:S(2)}) async-start(bf16[5,1536,1536]{2,0,1:T(8,128)(2,1)} %copy.96), calls=%async_computation.3 | async-start | bytes 75497472 | tf_op jit(solution)/shard_map/all_to_all | solution.py:211
  1465.9 617.8 %reduce-scatter.25.cloned.1.call-start = ((), (), s32[]{:S(2)}) async-start(), calls=%async_computation.22 | async-start | bytes 491520
  1471.4 643.0 %reduce-scatter.15.cloned.1.call-start = ((), (), s32[]{:S(2)}) async-start(), calls=%async_computation.14 | async-start | bytes 1966080 | tf_op jit(solution)/shard_map/reduce_scatter | solution.py:271
  1875.5 28.9 %copy-start.42 = (s32[4096]{0:T(1024)S(1)}, s32[4096]{0:T(1024)}, u32[]{:S(2)}) copy-start(s32[4096]{0:T(1024)} %copy-done.41) | copy-start | bytes 49156
  1998.5 147.2 %reduce-scatter.13.cloned.1.call-start = ((), (), s32[]{:S(2)}) async-start(), calls=%async_computation.13 | async-start | bytes 1966080 | tf_op jit(solution)/shard_map/reduce_scatter | solution.py:268
  2033.3 162.7 %reduce-scatter.17.cloned.1.call-start = ((), (), s32[]{:S(2)}) async-start(), calls=%async_computation.15 | async-start | bytes 5898240 | tf_op jit(solution)/shard_map/reduce_scatter | solution.py:274
  2040.8 205.8 %reduce-scatter.11.cloned.1.call-start = ((), (), s32[]{:S(2)}) async-start(), calls=%async_computation.12 | async-start | bytes 5898240 | tf_op jit(solution)/shard_map/reduce_scatter | solution.py:265
  2055.3 501.5 %all-gather.8.cloned.1.call-start = ((), (), s32[]{:S(2)}) async-start(), calls=%async_computation.21 | async-start | bytes 8847360 | tf_op jit(solution)/shard_map/all_gather | solution.py:300
  2058.1 581.2 %all-gather.6.cloned.1.call-start = ((), (), s32[]{:S(2)}) async-start(), calls=%async_computation.19 | async-start | bytes 8847360 | tf_op jit(solution)/shard_map/all_gather | solution.py:297
  2060.8 697.8 %all-gather.4.cloned.1.call-start = ((), (), s32[]{:S(2)}) async-start(), calls=%async_computation.17 | async-start | bytes 8847360 | tf_op jit(solution)/shard_map/all_gather | solution.py:294
  (52 other events, 466.9 us)
Sparse Core Ops, SparseCore 0:
  1300.4 252.2 reduce-scatter.22
  1556.8 250.2 reduce-scatter.20
  1811.2 250.1 reduce-scatter.18
  2063.8 19.9 reduce-scatter.24
  2086.1 28.1 reduce-scatter.14
  2117.5 28.1 reduce-scatter.12
  2148.2 47.8 reduce-scatter.16
  2198.8 47.8 reduce-scatter.10
  2248.8 246.0 all-gather.7
  2497.5 141.6 all-gather.5
  2642.0 116.5 all-gather.3
where the time goes:
time: 2790 us; the launch traced here: 2780 us
  waiting for transfers between devices  1130 us (41%)
  blocking collectives  840 us (30%)
  matrix products  339 us (12%)
  local copies, waits for them, and re-layouts  295 us (11%)
  other arithmetic  133 us (5%)
    all_to_all x1, waiting for transfers between devices, per_device(): lax.all_to_all(y_buf, 'ep', split_axis=1, concat_axis=0, tiled=True)  403 us
    all_to_all x1, waiting for transfers between devices, per_device(): lax.all_to_all(d_rows_held, 'ep', split_axis=1, concat_axis=0, tiled=True)  391 us
    psum x1, blocking collectives, per_device(): lax.psum((part_na, part_q, part_k, part_v, part_o, part_nf, part_r), 'rep')  310 us
    all_to_all x1, blocking collectives, per_device(): lax.all_to_all(send_buf, 'ep', split_axis=0, concat_axis=1, tiled=True)  262 us
    all_to_all x1, blocking collectives, per_device(): lax.all_to_all(d_send, 'ep', split_axis=0, concat_axis=1, tiled=True)  261 us
    all_gather x1, waiting for transfers between devices, per_device(): lax.all_gather(share_gate.astype(jnp.bfloat16), 'rep', axis=1, tiled=True)  108 us
    gather x2, local copies, waits for them, and re-layouts, unpack_rows(): return buffer.reshape(-1, width)[target].reshape(token_count, TOPK, width)  72.3 us
    all_gather x1, waiting for transfers between devices, per_device(): lax.all_gather(share_up.astype(jnp.bfloat16), 'rep', axis=1, tiled=True)  71 us
  transfers between devices with their start and end apart: 13, of which 10 were waited for; matrix products, arithmetic and copies ran while one was open for 14% of the time, Pallas kernels for 0%

commit v1 on v0

--- a/solution.py
+++ b/solution.py
@@ -13,6 +13,18 @@
 CAP = 384
 epsilon = 1e-06
 masked_value = -1e30
+
+
+def cut_along(array, dim, devices):
+    dims = array.shape
+    blocks = array.reshape(*dims[:dim], devices, dims[dim] // devices, *dims[dim + 1 :])
+    return jnp.moveaxis(blocks, dim, 0)
+
+
+def laid_out(blocks, dim):
+    lengths = list(blocks.shape[1:])
+    lengths[dim] *= blocks.shape[0]
+    return jnp.moveaxis(blocks, 0, dim).reshape(lengths)
 
 
 def rope_tables(token_count, width):
@@ -184,7 +196,14 @@
     slot_of = jnp.sum((jnp.cumsum(matches, 0) - 1) * matches, 1)
     target = flat_routes * CAP + slot_of
     send_buf = pack_rows(jnp.repeat(h_two, TOPK, axis=0), target, experts_all, width)
-    recv_rows = lax.all_to_all(send_buf, "ep", split_axis=0, concat_axis=1, tiled=True)
+    size, place = (lax.axis_size("ep"), lax.axis_index("ep"))
+    tiles = cut_along(send_buf, 0, size)
+    finished = [tiles[place]]
+    for step in range(1, size):
+        sent = tiles[place ^ step]
+        finished.append(lax.ppermute(sent, "ep", [(i, i ^ step) for i in range(size)]))
+    tiles = jnp.stack(finished)[place ^ jnp.arange(size)]
+    recv_rows = laid_out(tiles, 1)
     y_buf, gate_pre, up_pre, hidden = expert_forward(recv_rows, w_gate, w_up, w_down)
     back_y = lax.all_to_all(y_buf, "ep", split_axis=1, concat_axis=0, tiled=True)
     y_rows = unpack_rows(back_y, target, token_count, width)

time: 2790 us -> 2860 us (1.025)
  blocking collectives: 840 us -> 578 us
  waiting for transfers between devices: 1130 us -> 1380 us
  local copies, waits for them, and re-layouts: 295 us -> 349 us
    all_to_all x1 -> x0, blocking collectives: 262 us -> none  [per_device(): lax.all_to_all(send_buf, 'ep', split_axis=0, concat_axis=1, tiled=True)]
    ppermute x0 -> x3, waiting for transfers between devices: none -> 254 us  [per_device(): lax.ppermute(sent, 'ep', [(i, i ^ step) for i in range(size)])]
    all_gather x1, waiting for transfers between devices: 71 us -> 108 us  [per_device(): lax.all_gather(share_up.astype(jnp.bfloat16), 'rep', axis=1, tiled=True)]
    all_gather x1, waiting for transfers between devices: 108 us -> 71 us  [per_device(): lax.all_gather(share_gate.astype(jnp.bfloat16), 'rep', axis=1, tiled=True)]
    gather x0 -> x4, local copies, waits for them, and re-layouts: none -> 31.3 us  [per_device(): tiles = jnp.stack(finished)[place ^ jnp.arange(size)]]
  transfers between devices with their start and end apart: 13 -> 16, of which waited for: 10 -> 12; matrix products, arithmetic and copies ran while one was open for 14% -> 14% of each run, Pallas kernels for 0% -> 0%
where the time goes in v1:
time: 2860 us; the launch traced here: 2850 us
  waiting for transfers between devices  1380 us (48%)
  blocking collectives  578 us (20%)
  local copies, waits for them, and re-layouts  349 us (12%)
  matrix products  348 us (12%)
  other arithmetic  155 us (5%)
    all_to_all x1, waiting for transfers between devices, per_device(): lax.all_to_all(y_buf, 'ep', split_axis=1, concat_axis=0, tiled=True)  403 us
    all_to_all x1, waiting for transfers between devices, per_device(): lax.all_to_all(d_rows_held, 'ep', split_axis=1, concat_axis=0, tiled=True)  389 us
    psum x1, blocking collectives, per_device(): lax.psum((part_na, part_q, part_k, part_v, part_o, part_nf, part_r), 'rep')  310 us
    all_to_all x1, blocking collectives, per_device(): lax.all_to_all(d_send, 'ep', split_axis=0, concat_axis=1, tiled=True)  261 us
    ppermute x3, waiting for transfers between devices, per_device(): lax.ppermute(sent, 'ep', [(i, i ^ step) for i in range(size)])  254 us
    all_gather x1, waiting for transfers between devices, per_device(): lax.all_gather(share_up.astype(jnp.bfloat16), 'rep', axis=1, tiled=True)  108 us
    gather x2, local copies, waits for them, and re-layouts, unpack_rows(): return buffer.reshape(-1, width)[target].reshape(token_count, TOPK, width)  72.4 us
    all_gather x1, waiting for transfers between devices, per_device(): lax.all_gather(share_gate.astype(jnp.bfloat16), 'rep', axis=1, tiled=True)  71 us
  transfers between devices with their start and end apart: 16, of which 12 were waited for; matrix products, arithmetic and copies ran while one was open for 14% of the time, Pallas kernels for 0%

profile of v1, /device:TPU:0, one launch (start us, length us, event | category | flops | bytes accessed | tf_op | source)
XLA Modules:
  0.0 2852.9 jit_solution(13037813870920897509)
XLA Ops:
  69.9 32.2 %scatter_custom_fusion = bf16[7680,1536]{1,0:T(8,128)(2,1)} fusion(s32[4096]{0:T(1024)S(1)} %bitcast.211, bf16[]{:T(256)} %constant.130.clone.1, bf16[512,1536]{1,0:T(8,128)(2,1)S(1)} %multiply_convert_fusion.3), kind=kCustom, calls=%fused_computation.34 | custom fusion | bytes 25165826 | tf_op jit(solution)/shard_map/scatter | solution.py:135
  123.5 121.2 %collective-permute-done.1 = bf16[5,384,1536]{2,1,0:T(8,128)(2,1)S(1)} collective-permute-done((bf16[5,384,1536]{2,1,0:T(8,128)(2,1)S(1)}, bf16[5,384,1536]{2,1,0:T(8,128)(2,1)S(1)}, u32[]{:S(2)}, u32[]{:S(2)}) %collective-permute-start.1) | collective-permute-done | bytes 5898272 | tf_op jit(solution)/shard_map/ppermute | solution.py:204
  244.7 126.0 %collective-permute-done.2 = bf16[5,384,1536]{2,1,0:T(8,128)(2,1)S(1)} collective-permute-done((bf16[5,384,1536]{2,1,0:T(8,128)(2,1)S(1)}, bf16[5,384,1536]{2,1,0:T(8,128)(2,1)S(1)}, u32[]{:S(2)}, u32[]{:S(2)}) %collective-permute-start.2) | collective-permute-done | bytes 5898272 | tf_op jit(solution)/shard_map/ppermute | solution.py:204
  475.5 29.5 %multiply_convert_fusion.2 = (bf16[5,1536,512]{2,1,0:T(8,128)(2,1)}, f32[5,1536,512]{2,1,0:T(8,128)}) fusion(f32[5,1536,512]{2,1,0:T(8,128)} %fusion.73, bf16[5,1536,1536]{2,1,0:T(8,128)(2,1)} %bitcast.182, bf16[5,1536,512]{2,1,0:T(8,128)(2,1)} %param.22), kind=kOutput, calls=%fused_computation.28 | convolution fusion | flops 12103188480 | bytes 70778880 | tf_op jit(solution)/shard_map/erd,edf->erf/dot_general | solution.py:112
  525.1 27.3 copy.92
  568.0 402.9 %all-to-all-done = bf16[5,1536,1536]{2,0,1:T(8,128)(2,1)} async-done(((bf16[5,1536,1536]{2,0,1:T(8,128)(2,1)}), bf16[5,1536,1536]{2,0,1:T(8,128)(2,1)}, u32[]{:S(2)}, u32[]{:S(2)}) %all-to-all-start) | async-done | bytes 23592992 | tf_op jit(solution)/shard_map/all_to_all | solution.py:208
  970.9 28.9 %copy.93 = bf16[5,4,384,1536]{3,2,0,1:T(8,128)(2,1)} copy(bf16[5,4,384,1536]{3,0,2,1:T(8,128)(2,1)} %bitcast.26) | data formatting | bytes 47185920 | tf_op jit(solution)/shard_map/all_to_all | solution.py:208
  999.8 36.2 %gather_fusion = bf16[4096,1536]{1,0:T(8,128)(2,1)} fusion(bf16[7680,1536]{1,0:T(8,128)(2,1)} %bitcast.177, s32[4096]{0:T(1024)S(1)} %broadcast_clamp_fusion), kind=kCustom, calls=%fused_computation | custom fusion | bytes 25182208 | tf_op jit(solution)/shard_map/gather | solution.py:140
  1053.7 33.1 %scatter_custom_fusion.1 = bf16[7680,1536]{1,0:T(8,128)(2,1)} fusion(s32[4096]{0:T(1024)S(1)} %bitcast.213, bf16[4096,1536]{1,0:T(8,128)(2,1)} %fusion.3, bf16[]{:T(256)} %constant.130.clone.1), kind=kCustom, calls=%fused_computation.38 | custom fusion | bytes 23593472 | tf_op jit(solution)/shard_map/scatter | solution.py:135
  1086.7 261.4 %all_to_all.48 = bf16[20,384,1536]{2,1,0:T(8,128)(2,1)S(1)} all-to-all(bf16[20,384,1536]{2,1,0:T(8,128)(2,1)} %bitcast.179), channel_id=1, replica_groups=mesh['rep'=8,'ep'=4] {'ep'}, dimensions={0} | all-to-all | bytes 47185920 | tf_op jit(solution)/shard_map/all_to_all | solution.py:226
  1377.4 29.9 %multiply_convert_fusion = (bf16[5,1536,512]{2,1,0:T(8,128)(2,1)}, bf16[5,1536,512]{2,1,0:T(8,128)(2,1)}) fusion(f32[5,1536,512]{2,1,0:T(8,128)} %fusion.73, f32[5,1536,512]{2,1,0:T(8,128)} %get-tuple-element.146, bf16[5,1536,1536]{2,1,0:T(8,128)(2,1)} %bitcast.186, bf16[5,512,1536]{2,1,0:T(8,128)(2,1)} %param.23), kind=kOutput, calls=%fused_computation.26 | convolution fusion | flops 12130713600 | bytes 78643200 | tf_op jit(solution)/shard_map/erd,efd->erf/dot_general | solution.py:121
  1429.2 23.1 fusion.77
  1452.3 25.1 fusion.74
  1477.4 30.7 %add_convert_fusion = bf16[5,1536,1536]{2,1,0:T(8,128)(2,1)} fusion(f32[5,1536,1536]{2,1,0:T(8,128)} %fusion.74, bf16[5,1536,512]{2,1,0:T(8,128)(2,1)} %get-tuple-element.120, bf16[5,1536,512]{2,1,0:T(8,128)(2,1)} %param.22), kind=kOutput, calls=%fused_computation.7 | convolution fusion | flops 12103188480 | bytes 86507520 | tf_op jit(solution)/shard_map/erf,edf->erd/dot_general | solution.py:130
  1508.1 27.3 copy.96
  1565.2 388.7 %all-to-all-done.2 = bf16[5,1536,1536]{2,0,1:T(8,128)(2,1)} async-done(((bf16[5,1536,1536]{2,0,1:T(8,128)(2,1)}), bf16[5,1536,1536]{2,0,1:T(8,128)(2,1)}, u32[]{:S(2)}, u32[]{:S(2)}) %all-to-all-start.2) | async-done | bytes 23592992 | tf_op jit(solution)/shard_map/all_to_all | solution.py:230
  1953.9 28.7 %copy.97 = bf16[5,4,384,1536]{3,2,0,1:T(8,128)(2,1)} copy(bf16[5,4,384,1536]{3,0,2,1:T(8,128)(2,1)} %bitcast.37) | data formatting | bytes 47185920 | tf_op jit(solution)/shard_map/all_to_all | solution.py:230
  1982.7 36.3 %gather_fusion.1 = bf16[4096,1536]{1,0:T(8,128)(2,1)} fusion(bf16[7680,1536]{1,0:T(8,128)(2,1)} %bitcast.176, s32[4096]{0:T(1024)S(1)} %copy-done.43), kind=kCustom, calls=%fused_computation.1 | custom fusion | bytes 25182208 | tf_op jit(solution)/shard_map/gather | solution.py:140
  2190.7 31.3 %reduce-scatter.13.cloned.1.call-done = bf16[384,512]{1,0:T(8,128)(2,1)} async-done(((bf16[1536,512]{1,0:T(8,128)(2,1)}), bf16[384,512]{1,0:T(8,128)(2,1)}) %reduce-scatter.13.cloned.1.call-update) | async-done | bytes 393232 | tf_op jit(solution)/shard_map/reduce_scatter | solution.py:287
  2222.0 50.4 %reduce-scatter.11.cloned.1.call-done = bf16[384,1536]{1,0:T(8,128)(2,1)} async-done(((bf16[1536,1536]{1,0:T(8,128)(2,1)}), bf16[384,1536]{1,0:T(8,128)(2,1)}) %reduce-scatter.11.cloned.1.call-update) | async-done | bytes 1179664 | tf_op jit(solution)/shard_map/reduce_scatter | solution.py:284
  2272.4 50.6 %reduce-scatter.17.cloned.1.call-done = bf16[384,1536]{1,0:T(8,128)(2,1)} async-done(((bf16[1536,1536]{1,0:T(8,128)(2,1)}), bf16[384,1536]{1,0:T(8,128)(2,1)}) %reduce-scatter.17.cloned.1.call-update) | async-done | bytes 1179664 | tf_op jit(solution)/shard_map/reduce_scatter | solution.py:293
  2322.9 310.2 %all-reduce.5 = (f32[384]{0:T(512)}, f32[384,1536]{1,0:T(8,128)}, f32[384,512]{1,0:T(8,128)}, f32[384,512]{1,0:T(8,128)}, f32[384,1536]{1,0:T(8,128)}, /*index=5*/f32[384]{0:T(512)}, f32[384,20]{0,1:T(8,128)}) all-reduce(f32[384]{0:T(512)S(1)} %get-tuple-element.154, ...), channel_id=1, replica_groups=mesh['rep'=8,'ep'=4] {'rep'}, use_global_device_ids=true, to_apply=%region_21.22 | all-reduce | flops 1581312 | bytes 9489408 | tf_op jit(solution)/shard_map/psum | solution.py:304
  2644.6 71.0 %all-gather.4.cloned.1.call-done = bf16[5,1536,512]{2,1,0:T(8,128)(2,1)} async-done(((bf16[5,192,512]{2,1,0:T(8,128)(2,1)}), bf16[5,1536,512]{2,1,0:T(8,128)(2,1)}) %all-gather.4.cloned.1.call-update) | async-done | bytes 7864336 | tf_op jit(solution)/shard_map/all_gather | solution.py:313
  2727.2 107.8 %all-gather.6.cloned.1.call-done = bf16[5,1536,512]{2,1,0:T(8,128)(2,1)} async-done(((bf16[5,192,512]{2,1,0:T(8,128)(2,1)}), bf16[5,1536,512]{2,1,0:T(8,128)(2,1)}) %all-gather.6.cloned.1.call-update) | async-done | bytes 7864336 | tf_op jit(solution)/shard_map/all_gather | solution.py:316
  (267 shorter events, 527.3 us)
Async XLA Ops:
  60.2 41.9 %copy-start.52 = (f32[512]{0:T(512)}, f32[512]{0:T(512)S(1)}, u32[]{:S(2)}) copy-start(f32[512]{0:T(512)S(1)} %add_rsqrt_fusion) | copy-start | bytes 6148
  60.3 41.9 %copy-start.44 = (f32[1536]{0:T(1024)}, f32[1536]{0:T(1024)S(1)}, u32[]{:S(2)}) copy-start(f32[1536]{0:T(1024)S(1)} %convert_element_type.213) | copy-start | bytes 18436
  67.7 34.5 %copy-start.48 = (s32[4096,1]{0,1:T(1,128)}, s32[4096,1]{0,1:T(1,128)S(1)}, u32[]{:S(2)}) copy-start(s32[4096,1]{0,1:T(1,128)S(1)} %compare_select_fusion) | copy-start | bytes 49156
  69.9 32.2 %copy-start.2 = (bf16[512,1536]{1,0:T(8,128)(2,1)}, bf16[512,1536]{1,0:T(8,128)(2,1)S(1)}, u32[]{:S(2)}) copy-start(bf16[512,1536]{1,0:T(8,128)(2,1)S(1)} %multiply_convert_fusion.3) | copy-start | bytes 4718596
  113.8 9.7 collective-permute-start
  114.2 130.4 %collective-permute-start.1 = (bf16[5,384,1536]{2,1,0:T(8,128)(2,1)S(1)}, bf16[5,384,1536]{2,1,0:T(8,128)(2,1)S(1)}, u32[]{:S(2)}, u32[]{:S(2)}) collective-permute-start(bf16[5,384,1536]{2,1,0:T(8,128)(2,1)S(1)} %get-tuple-element.127), channel_id=1, source_target_pairs={{0,2},{1,3},{2,0},{3,1},{4,6},{5,7},{6,4},{7,5},{8,10},{9,11},{10,... | collective-permute-start | bytes 17694728 | tf_op jit(solution)/shard_map/ppermute | solution.py:204
  116.7 254.0 %collective-permute-start.2 = (bf16[5,384,1536]{2,1,0:T(8,128)(2,1)S(1)}, bf16[5,384,1536]{2,1,0:T(8,128)(2,1)S(1)}, u32[]{:S(2)}, u32[]{:S(2)}) collective-permute-start(bf16[5,384,1536]{2,1,0:T(8,128)(2,1)S(1)} %get-tuple-element.126), channel_id=1, source_target_pairs={{0,3},{1,2},{2,1},{3,0},{4,7},{5,6},{6,5},{7,4},{8,11},{9,10},{10,... | collective-permute-start | bytes 17694728 | tf_op jit(solution)/shard_map/ppermute | solution.py:204
  552.4 418.4 %all-to-all-start = ((bf16[5,1536,1536]{2,0,1:T(8,128)(2,1)}), bf16[5,1536,1536]{2,0,1:T(8,128)(2,1)}, u32[]{:S(2)}, u32[]{:S(2)}) async-start(bf16[5,1536,1536]{2,0,1:T(8,128)(2,1)} %copy.92), calls=%async_computation | async-start | bytes 75497472 | tf_op jit(solution)/shard_map/all_to_all | solution.py:208
  563.1 1570.2 %reduce-scatter.23.cloned.1.call-start = ((), (), s32[]{:S(2)}) async-start(), calls=%async_computation.19 | async-start | bytes 17694720 | tf_op jit(solution)/shard_map/reduce_scatter | solution.py:310
  567.3 432.5 %copy-start.50 = (f32[512]{0:T(512)}, f32[512]{0:T(512)S(1)}, u32[]{:S(2)}) copy-start(f32[512]{0:T(512)S(1)} %get-tuple-element.147) | copy-start | bytes 6148
  567.4 432.4 %copy-start.54 = (f32[512]{0:T(512)}, f32[512]{0:T(512)S(1)}, u32[]{:S(2)}) copy-start(f32[512]{0:T(512)S(1)} %fusion.47) | copy-start | bytes 6148
  567.9 431.9 %copy-start.42 = (s32[4096]{0:T(1024)}, s32[4096]{0:T(1024)S(1)}, u32[]{:S(2)}) copy-start(s32[4096]{0:T(1024)S(1)} %broadcast_clamp_fusion) | copy-start | bytes 49156
  999.8 36.2 %copy-start.10 = (bf16[512,1536]{1,0:T(8,128)(2,1)S(1)}, bf16[512,1536]{1,0:T(8,128)(2,1)}, u32[]{:S(2)}) copy-start(bf16[512,1536]{1,0:T(8,128)(2,1)} %param.25) | copy-start | bytes 4718596
  1377.4 758.7 %reduce-scatter.19.cloned.1.call-start = ((), (), s32[]{:S(2)}) async-start(), calls=%async_computation.15 | async-start | bytes 17694720 | tf_op jit(solution)/shard_map/reduce_scatter | solution.py:308
  1429.2 709.6 %reduce-scatter.21.cloned.1.call-start = ((), (), s32[]{:S(2)}) async-start(), calls=%async_computation.17 | async-start | bytes 17694720 | tf_op jit(solution)/shard_map/reduce_scatter | solution.py:309
  1535.5 418.4 %all-to-all-start.2 = ((bf16[5,1536,1536]{2,0,1:T(8,128)(2,1)}), bf16[5,1536,1536]{2,0,1:T(8,128)(2,1)}, u32[]{:S(2)}, u32[]{:S(2)}) async-start(bf16[5,1536,1536]{2,0,1:T(8,128)(2,1)} %copy.96), calls=%async_computation.2 | async-start | bytes 75497472 | tf_op jit(solution)/shard_map/all_to_all | solution.py:230
  1546.2 613.9 %reduce-scatter.25.cloned.1.call-start = ((), (), s32[]{:S(2)}) async-start(), calls=%async_computation.21 | async-start | bytes 491520
  1551.6 639.0 %reduce-scatter.15.cloned.1.call-start = ((), (), s32[]{:S(2)}) async-start(), calls=%async_computation.13 | async-start | bytes 1966080 | tf_op jit(solution)/shard_map/reduce_scatter | solution.py:290
  2077.0 145.0 %reduce-scatter.13.cloned.1.call-start = ((), (), s32[]{:S(2)}) async-start(), calls=%async_computation.12 | async-start | bytes 1966080 | tf_op jit(solution)/shard_map/reduce_scatter | solution.py:287
  2111.9 160.5 %reduce-scatter.11.cloned.1.call-start = ((), (), s32[]{:S(2)}) async-start(), calls=%async_computation.11 | async-start | bytes 5898240 | tf_op jit(solution)/shard_map/reduce_scatter | solution.py:284
  2126.0 197.0 %reduce-scatter.17.cloned.1.call-start = ((), (), s32[]{:S(2)}) async-start(), calls=%async_computation.14 | async-start | bytes 5898240 | tf_op jit(solution)/shard_map/reduce_scatter | solution.py:293
  2133.2 499.9 %all-gather.8.cloned.1.call-start = ((), (), s32[]{:S(2)}) async-start(), calls=%async_computation.20 | async-start | bytes 8847360 | tf_op jit(solution)/shard_map/all_gather | solution.py:319
  2136.0 579.6 %all-gather.4.cloned.1.call-start = ((), (), s32[]{:S(2)}) async-start(), calls=%async_computation.16 | async-start | bytes 8847360 | tf_op jit(solution)/shard_map/all_gather | solution.py:313
  2138.7 696.3 %all-gather.6.cloned.1.call-start = ((), (), s32[]{:S(2)}) async-start(), calls=%async_computation.18 | async-start | bytes 8847360 | tf_op jit(solution)/shard_map/all_gather | solution.py:316
  (57 other events, 567.2 us)
Sparse Core Ops, SparseCore 0:
  1377.5 251.4 reduce-scatter.22
  1633.2 250.1 reduce-scatter.18
  1887.6 250.1 reduce-scatter.20
  2140.1 19.8 reduce-scatter.24
  2162.5 28.1 reduce-scatter.14
  2193.8 28.1 reduce-scatter.12
  2224.5 47.8 reduce-scatter.10
  2275.1 47.8 reduce-scatter.16
  2325.1 246.0 all-gather.7
  2573.8 141.7 all-gather.3
  2718.4 116.5 all-gather.5
